TPU v7x, 32 devices: a whole 2x2x4 slice. The times are simulated.
32 devices in a mesh: dp: 2 (over y), fsdp: 16 (over z, x, core).
Axes of the slice: x: 2, y: 2, z: 4, core: 2. Of those that a mesh axis runs over, the one named last changes fastest.
Arguments:
- tokens: bfloat16 [32768, 1024], P(('dp', 'fsdp')), may hold values from -12 to 12
- ln_gain: bfloat16 [1024], P(('dp', 'fsdp')), may hold values from 0.099609375 to 1.8984375
- ln_bias: bfloat16 [1024], P(('dp', 'fsdp')), may hold values from -1.75 to 1.75
- qkv_weight: bfloat16 [1024, 3072], P(('dp', 'fsdp')), may hold values from -0.1875 to 0.1875
- qkv_bias: bfloat16 [3072], P(('dp', 'fsdp')), may hold values from -1.75 to 1.75
- out_weight: bfloat16 [1024, 1024], P(('dp', 'fsdp')), may hold values from -0.75 to 0.75
- out_bias: bfloat16 [1024], P(('dp', 'fsdp')), may hold values from -1.75 to 1.75
- fc1_weight: bfloat16 [1024, 4096], P(('dp', 'fsdp')), may hold values from -0.1875 to 0.1875
- fc1_bias: bfloat16 [4096], P(('dp', 'fsdp')), may hold values from -3 to 3
- fc2_weight: bfloat16 [4096, 1024], P(('dp', 'fsdp')), may hold values from -0.09375 to 0.09375
- fc2_bias: bfloat16 [1024], P(('dp', 'fsdp')), may hold values from -1.75 to 1.75
- cotangent: float32 [32768, 1024], P(('dp', 'fsdp')), may hold values from -6 to 6
- doc_lengths: int32 [32, 4], P(('dp', 'fsdp')), may hold values from 1 to 512, 1024 in all within a row
- node_seeds: int32 [64, 64], replicated, may hold values from 0 to 1023
- node_weights: int32 [64], replicated, may hold values from 1 to 16
Outputs:
- output: float32 [32768, 1024], P(('dp', 'fsdp'))
- input_grad: float32 [32768, 1024], P(('dp', 'fsdp'))
- g_ln_gain: float32 [1024], P(('dp', 'fsdp'))
- g_ln_bias: float32 [1024], P(('dp', 'fsdp'))
- g_qkv_weight: float32 [1024, 3072], P(('dp', 'fsdp'))
- g_qkv_bias: float32 [3072], P(('dp', 'fsdp'))
- g_out_weight: float32 [1024, 1024], P(('dp', 'fsdp'))
- g_out_bias: float32 [1024], P(('dp', 'fsdp'))
- g_fc1_weight: float32 [1024, 4096], P(('dp', 'fsdp'))
- g_fc1_bias: float32 [4096], P(('dp', 'fsdp'))
- g_fc2_weight: float32 [4096, 1024], P(('dp', 'fsdp'))
- g_fc2_bias: float32 [1024], P(('dp', 'fsdp'))
Inputs may be any that keep to these rules, and one draw needn't show every extreme that they name: `doc_lengths`: each row holds the lengths of 4 documents that fill one sequence of 1024 tokens; its longest document has exactly 512 tokens.
All inputs are finite; a program needn't handle non-finite values.
Results may differ from a plain program's by a relative error of at most 0.0093.
Values may be sent and summed in bfloat16 or wider, within the bound.
No kernel may reach another device: no remote copies, remote signals or barrier semaphores. Data moves between devices by JAX's collectives and lax.ppermute only.
A program may use at most 256 MiB of HBM per device.

v0:
```python
import math
import jax
import jax.numpy as jnp
from jax import lax
from jax.sharding import PartitionSpec as P

D = 1024
HEADS = 16
HD = 64
ROT = 16
LEN = 1024
DOCS = 4
feature_scale = 0.2
epsilon = 1e-05
precise = lax.Precision.HIGHEST


def tables(node_seeds, node_weights):
    width = node_seeds.shape[1]
    uniform_pts = (node_seeds.astype(jnp.float32) + 0.5) / 1024.0
    nodes = math.sqrt(2.0) * lax.erf_inv(2.0 * uniform_pts - 1.0)
    order = jnp.arange(width).astype(jnp.float32)
    scales = jnp.where(order[:, None] == 0.0, math.sqrt(1.0 / width), math.sqrt(2.0 / width))
    basis = scales * jnp.cos(
        math.pi * (2.0 * order[None, :] + 1.0) * order[:, None] / (2.0 * width)
    )
    projection = jnp.dot(nodes, basis, precision=precise)
    weights_float = node_weights.astype(jnp.float32)
    return (projection, weights_float / jnp.sum(weights_float))


def layout(lengths):
    ends = jnp.cumsum(lengths)
    starts = ends - lengths
    places = jnp.arange(LEN, dtype=jnp.int32)
    doc_ids = jnp.sum((places[:, None] >= ends[None, :]).astype(jnp.int32), axis=1)
    owners = doc_ids[:, None] == jnp.arange(DOCS, dtype=jnp.int32)[None, :]
    begins = jnp.sum(jnp.where(owners, starts[None, :], 0), axis=1)
    return (doc_ids, (places - begins).astype(jnp.float32))


def rotary(positions):
    half_rot = ROT // 2
    freqs = 10000.0 ** (-2.0 * jnp.arange(half_rot).astype(jnp.float32) / ROT)
    angles = positions[:, None] * freqs[None, :]
    return (jnp.cos(angles), jnp.sin(angles))


def rotate(heads, cos_table, sin_table):
    half_rot = cos_table.shape[1]
    first = heads[..., :half_rot]
    second = heads[..., half_rot : 2 * half_rot]
    rest = heads[..., 2 * half_rot :]
    cos_wide = cos_table[:, None, :]
    sin_wide = sin_table[:, None, :]
    return jnp.concatenate(
        [first * cos_wide - second * sin_wide, second * cos_wide + first * sin_wide, rest], axis=-1
    )


def features(heads, cos_table, sin_table, projection):
    turned = feature_scale * rotate(heads, cos_table, sin_table)
    exponent = jnp.einsum("lhd,md->lhm", turned, projection, precision=precise)
    exponent = exponent - 0.5 * jnp.sum(turned * turned, axis=-1, keepdims=True)
    return jnp.exp(exponent)


def plain_dot(left, right):
    return jnp.dot(left, right, preferred_element_type=jnp.float32)


def outer_sum(left, right):
    return lax.dot_general(
        left, right, (((0,), (0,)), ((), ())), preferred_element_type=jnp.float32
    )


def back_proj(left, right):
    return lax.dot_general(
        left, right, (((1,), (1,)), ((), ())), preferred_element_type=jnp.float32
    )


def gelu_slope(upper):
    return 0.5 * (1.0 + lax.erf(upper / math.sqrt(2.0))) + upper * jnp.exp(
        -0.5 * upper * upper
    ) / math.sqrt(2.0 * math.pi)


def block_mask(doc_ids, first, block):
    places = jnp.arange(doc_ids.shape[0], dtype=jnp.int32)
    rows_here = places[first : first + block]
    same_doc = doc_ids[first : first + block, None] == doc_ids[None, :]
    return same_doc & (rows_here[:, None] >= places[None, :])


def attend(fq_low, fk_low, values_low, doc_ids):
    seq_len = doc_ids.shape[0]
    block = min(512, seq_len)
    outputs = []
    denoms = []
    for first in range(0, seq_len, block):
        mask = block_mask(doc_ids, first, block)
        raw = jnp.einsum(
            "qhm,khm->hqk",
            fq_low[first : first + block],
            fk_low,
            preferred_element_type=jnp.float32,
        )
        scores = jnp.where(mask[None], raw, 0.0)
        denom = jnp.sum(scores, axis=-1)
        numer = jnp.einsum(
            "hqk,khd->qhd",
            scores.astype(jnp.bfloat16),
            values_low,
            preferred_element_type=jnp.float32,
        )
        outputs.append(numer / denom.T[:, :, None])
        denoms.append(denom)
    return (jnp.concatenate(outputs, axis=0), jnp.concatenate(denoms, axis=1))


def attend_back(fq_low, fk_low, values_low, doc_ids, grad_out, attn_out, denom):
    seq_len = doc_ids.shape[0]
    block = min(512, seq_len)
    d_values = jnp.zeros(values_low.shape, jnp.float32)
    d_fk = jnp.zeros(fk_low.shape, jnp.float32)
    d_fq_parts = []
    for first in range(0, seq_len, block):
        mask = block_mask(doc_ids, first, block)
        fq_block = fq_low[first : first + block]
        raw = jnp.einsum("qhm,khm->hqk", fq_block, fk_low, preferred_element_type=jnp.float32)
        scores_low = jnp.where(mask[None], raw, 0.0).astype(jnp.bfloat16)
        den_block = denom[:, first : first + block].T
        grad_block = grad_out[first : first + block]
        d_num_low = (grad_block / den_block[:, :, None]).astype(jnp.bfloat16)
        d_denom = -jnp.sum(grad_block * attn_out[first : first + block], axis=-1) / den_block
        d_prod = jnp.einsum(
            "qhd,khd->hqk", d_num_low, values_low, preferred_element_type=jnp.float32
        )
        d_scores_low = jnp.where(
            mask[None],
            (d_prod + d_denom.T[:, :, None]).astype(jnp.bfloat16),
            jnp.zeros((), jnp.bfloat16),
        )
        d_values = d_values + jnp.einsum(
            "hqk,qhd->khd", scores_low, d_num_low, preferred_element_type=jnp.float32
        )
        d_fq_parts.append(
            jnp.einsum("hqk,khm->qhm", d_scores_low, fk_low, preferred_element_type=jnp.float32)
        )
        d_fk = d_fk + jnp.einsum(
            "hqk,qhm->khm", d_scores_low, fq_block, preferred_element_type=jnp.float32
        )
    return (jnp.concatenate(d_fq_parts, axis=0), d_fk, d_values)


def shards(
    tokens,
    ln_gain,
    ln_bias,
    qkv_weight,
    qkv_bias,
    out_weight,
    out_bias,
    fc1_weight,
    fc1_bias,
    fc2_weight,
    fc2_bias,
    cotangent,
    doc_lengths,
    node_seeds,
    node_weights,
):
    whole = (
        lax.all_gather(ln_gain, ("dp", "fsdp"), axis=0, tiled=True),
        lax.all_gather(ln_bias, ("dp", "fsdp"), axis=0, tiled=True),
        lax.all_gather(qkv_weight, ("dp", "fsdp"), axis=0, tiled=True),
        lax.all_gather(qkv_bias, ("dp", "fsdp"), axis=0, tiled=True),
        lax.all_gather(out_weight, ("dp", "fsdp"), axis=0, tiled=True),
        lax.all_gather(out_bias, ("dp", "fsdp"), axis=0, tiled=True),
        lax.all_gather(fc1_weight, ("dp", "fsdp"), axis=0, tiled=True),
        lax.all_gather(fc1_bias, ("dp", "fsdp"), axis=0, tiled=True),
        lax.all_gather(fc2_weight, ("dp", "fsdp"), axis=0, tiled=True),
        lax.all_gather(fc2_bias, ("dp", "fsdp"), axis=0, tiled=True),
    )
    (
        norm_gain,
        norm_shift,
        joint_weight,
        joint_bias,
        attn_weight,
        attn_bias,
        up_weight,
        up_bias,
        down_weight,
        down_bias,
    ) = whole
    rows_x = tokens.astype(jnp.float32)
    center = rows_x - jnp.mean(rows_x, axis=-1, keepdims=True)
    inv_std = lax.rsqrt(jnp.mean(center * center, axis=-1, keepdims=True) + epsilon)
    normed = center * inv_std
    hidden = normed * norm_gain.astype(jnp.float32) + norm_shift.astype(jnp.float32)
    hidden_low = hidden.astype(jnp.bfloat16)
    mixed = plain_dot(hidden_low, joint_weight) + joint_bias.astype(jnp.float32)
    upper = plain_dot(hidden_low, up_weight) + up_bias.astype(jnp.float32)
    act_low = jax.nn.gelu(upper, approximate=False).astype(jnp.bfloat16)
    branch_mlp = plain_dot(act_low, down_weight) + down_bias.astype(jnp.float32)
    projection, quad = tables(node_seeds, node_weights)
    seq = 0
    doc_ids, positions = layout(doc_lengths[seq])
    cos_table, sin_table = rotary(positions)
    query_heads = mixed[:, :D].reshape(LEN, HEADS, HD)
    key_heads = mixed[:, D : 2 * D].reshape(LEN, HEADS, HD)
    values_low = mixed[:, 2 * D :].reshape(LEN, HEADS, HD).astype(jnp.bfloat16)
    fq_low = (features(query_heads, cos_table, sin_table, projection) * quad).astype(jnp.bfloat16)
    fk_low = features(key_heads, cos_table, sin_table, projection).astype(jnp.bfloat16)
    attn_seq, denom = attend(fq_low, fk_low, values_low, doc_ids)
    kept = [
        (
            doc_ids,
            cos_table,
            sin_table,
            query_heads,
            key_heads,
            values_low,
            fq_low,
            fk_low,
            attn_seq,
            denom,
        )
    ]
    attn_parts = attn_seq.reshape(LEN, D)
    attn_low = attn_parts.astype(jnp.bfloat16)
    branch_attn = plain_dot(attn_low, attn_weight) + attn_bias.astype(jnp.float32)
    output = rows_x + branch_attn + branch_mlp
    again = (
        lax.all_gather(ln_gain, ("dp", "fsdp"), axis=0, tiled=True),
        lax.all_gather(ln_bias, ("dp", "fsdp"), axis=0, tiled=True),
        lax.all_gather(qkv_weight, ("dp", "fsdp"), axis=0, tiled=True),
        lax.all_gather(qkv_bias, ("dp", "fsdp"), axis=0, tiled=True),
        lax.all_gather(out_weight, ("dp", "fsdp"), axis=0, tiled=True),
        lax.all_gather(out_bias, ("dp", "fsdp"), axis=0, tiled=True),
        lax.all_gather(fc1_weight, ("dp", "fsdp"), axis=0, tiled=True),
        lax.all_gather(fc1_bias, ("dp", "fsdp"), axis=0, tiled=True),
        lax.all_gather(fc2_weight, ("dp", "fsdp"), axis=0, tiled=True),
        lax.all_gather(fc2_bias, ("dp", "fsdp"), axis=0, tiled=True),
    )
    (
        norm_gain,
        norm_shift,
        joint_weight,
        joint_bias,
        attn_weight,
        attn_bias,
        up_weight,
        up_bias,
        down_weight,
        down_bias,
    ) = again
    dy_low = cotangent.astype(jnp.bfloat16)
    dy_sums = jnp.sum(dy_low.astype(jnp.float32), axis=0)
    g_down_weight = outer_sum(act_low, dy_low)
    g_attn_weight = outer_sum(attn_low, dy_low)
    d_up_low = (back_proj(dy_low, down_weight) * gelu_slope(upper)).astype(jnp.bfloat16)
    g_up_weight = outer_sum(hidden_low, d_up_low)
    g_up_bias = jnp.sum(d_up_low.astype(jnp.float32), axis=0)
    d_attn = back_proj(dy_low, attn_weight)
    seq = 0
    (
        doc_ids,
        cos_table,
        sin_table,
        query_heads,
        key_heads,
        values_low,
        fq_low,
        fk_low,
        attn_seq,
        denom,
    ) = kept[seq]
    grad_out = d_attn.reshape(LEN, HEADS, HD)
    d_fq, d_fk, d_values = attend_back(
        fq_low, fk_low, values_low, doc_ids, grad_out, attn_seq, denom
    )

    def feature_pair(query_part, key_part):
        return (
            features(query_part, cos_table, sin_table, projection) * quad,
            features(key_part, cos_table, sin_table, projection),
        )

    unused, pull = jax.vjp(feature_pair, query_heads, key_heads)
    d_queries, d_keys = pull((d_fq, d_fk))
    d_mixed_parts = jnp.concatenate(
        [d_queries.reshape(LEN, D), d_keys.reshape(LEN, D), d_values.reshape(LEN, D)], axis=1
    )
    d_mixed_low = d_mixed_parts.astype(jnp.bfloat16)
    g_joint_weight = outer_sum(hidden_low, d_mixed_low)
    g_joint_bias = jnp.sum(d_mixed_low.astype(jnp.float32), axis=0)
    d_hidden = back_proj(d_mixed_low, joint_weight) + back_proj(d_up_low, up_weight)
    g_norm_gain = jnp.sum(d_hidden * normed, axis=0)
    g_norm_shift = jnp.sum(d_hidden, axis=0)
    d_normed = d_hidden * norm_gain.astype(jnp.float32)
    mean_grad = jnp.mean(d_normed, axis=-1, keepdims=True)
    mean_cross = jnp.mean(d_normed * normed, axis=-1, keepdims=True)
    input_grad = cotangent + inv_std * (d_normed - mean_grad - normed * mean_cross)
    reduced = (
        lax.psum_scatter(g_norm_gain, ("dp", "fsdp"), scatter_dimension=0, tiled=True),
        lax.psum_scatter(g_norm_shift, ("dp", "fsdp"), scatter_dimension=0, tiled=True),
        lax.psum_scatter(g_joint_weight, ("dp", "fsdp"), scatter_dimension=0, tiled=True),
        lax.psum_scatter(g_joint_bias, ("dp", "fsdp"), scatter_dimension=0, tiled=True),
        lax.psum_scatter(g_attn_weight, ("dp", "fsdp"), scatter_dimension=0, tiled=True),
        lax.psum_scatter(dy_sums, ("dp", "fsdp"), scatter_dimension=0, tiled=True),
        lax.psum_scatter(g_up_weight, ("dp", "fsdp"), scatter_dimension=0, tiled=True),
        lax.psum_scatter(g_up_bias, ("dp", "fsdp"), scatter_dimension=0, tiled=True),
        lax.psum_scatter(g_down_weight, ("dp", "fsdp"), scatter_dimension=0, tiled=True),
        lax.psum_scatter(dy_sums, ("dp", "fsdp"), scatter_dimension=0, tiled=True),
    )
    return (
        output,
        input_grad,
        reduced[0],
        reduced[1],
        reduced[2],
        reduced[3],
        reduced[4],
        reduced[5],
        reduced[6],
        reduced[7],
        reduced[8],
        reduced[9],
    )


def solution(mesh):
    in_specs = (
        P(("dp", "fsdp"), None),
        P(("dp", "fsdp")),
        P(("dp", "fsdp")),
        P(("dp", "fsdp"), None),
        P(("dp", "fsdp")),
        P(("dp", "fsdp"), None),
        P(("dp", "fsdp")),
        P(("dp", "fsdp"), None),
        P(("dp", "fsdp")),
        P(("dp", "fsdp"), None),
        P(("dp", "fsdp")),
        P(("dp", "fsdp"), None),
        P(("dp", "fsdp"), None),
        P(),
        P(),
    )
    out_specs = (
        P(("dp", "fsdp"), None),
        P(("dp", "fsdp"), None),
        P(("dp", "fsdp")),
        P(("dp", "fsdp")),
        P(("dp", "fsdp"), None),
        P(("dp", "fsdp")),
        P(("dp", "fsdp"), None),
        P(("dp", "fsdp")),
        P(("dp", "fsdp"), None),
        P(("dp", "fsdp")),
        P(("dp", "fsdp"), None),
        P(("dp", "fsdp")),
    )
    return jax.shard_map(shards, mesh=mesh, in_specs=in_specs, out_specs=out_specs, check_vma=False)
```

profile of v0, /device:TPU:4, one launch (start us, length us, event | category | flops | bytes accessed | tf_op | source)
XLA Modules:
  0.0 982.5 jit_solution(15464834726994419618)
XLA Ops:
  18.3 42.6 %all-reduce.17 = (bf16[3072]{0:T(1024)(128)(2,1)S(1)}, bf16[1024]{0:T(1024)(128)(2,1)S(1)}, bf16[1024]{0:T(1024)(128)(2,1)S(1)}, bf16[1024]{0:T(1024)(128)(2,1)}, bf16[1024]{0:T(1024)(128)(2,1)}) all-reduce(bf16[3072]{0:T(1024)(128)(2,1)S(1)} %dynamic-update-slice.2, ...), channel_id=1, replica_groups=mesh['dp'=2,'fsdp'=16] {'dp','fsdp'}, use_global_device_ids=true, to_apply=%add.8 | all-reduce | flops 7168 | bytes 28672
  78.0 62.4 %all-gather.6.cloned.1.call-done = bf16[1024,3072]{1,0:T(8,128)(2,1)} async-done(((bf16[32,3072]{1,0:T(8,128)(2,1)}), bf16[1024,3072]{1,0:T(8,128)(2,1)}) %all-gather.6.cloned.1.call-update) | async-done | bytes 6291472 | tf_op jit(solution)/shard_map/all_gather | solution.py:178
  140.4 9.0 broadcast_add_fusion
  206.5 13.2 %bitcast_divide_fusion.1 = f32[512,16,64]{0,2,1:T(8,128)} fusion(bf16[1024,16,64]{0,2,1:T(8,128)(2,1)} %bitcast.93, bf16[16,512,1024]{2,1,0:T(8,128)(2,1)} %get-tuple-element.61, pred[512,1024]{1,0:T(8,128)(4,1)} %get-tuple-element.50, f32[512,16]{0,1:T(8,128)S(1)} %bitcast.104), kind=kOutput, calls=%fused_computation.87 | convolution fusion | flops 1082654720 | bytes 21528576 | tf_op jit(solution)/shard_map/hqk,khd->qhd/dot_general | solution.py:112
  219.7 11.8 %multiply_reduce_fusion.3 = (f32[512,16]{0,1:T(8,128)S(1)}, f32[512,16]{0,1:T(8,128)S(1)}, bf16[512,16,64]{0,2,1:T(8,128)(2,1)S(1)}, bf16[512,16,64]{0,2,1:T(8,128)(2,1)S(1)}) fusion(f32[1024,1024]{0,1:T(8,128)} %copy-done.21, f32[512,16,64]{0,2,1:T(8,128)} %bitcast_divide_fusion.1, f32[512,16]{0,1:T(8,128)S(1)} %bitcast.101, ...), kind=kOutput, calls=%fused_computation.88 | convolution fusion | flops 1085784064 | bytes 27885568 | tf_op jit(solution)/shard_map/hqk,khd->qhd/dot_general | solution.py:112
  238.2 11.5 %fusion.9 = bf16[16,512,1024]{2,1,0:T(8,128)(2,1)} fusion(f32[16,512]{1,0:T(8,128)S(1)} %bitcast_divide_fusion.3, pred[512,1024]{1,0:T(8,128)(4,1)} %get-tuple-element.50, bf16[1024,16,64]{0,2,1:T(8,128)(2,1)} %bitcast.95, f32[512,16,64]{0,2,1:T(8,128)} %bitcast.99, f32[512,16]{0,1:T(8,128)S(1)} %bitcast.105), kind=kOutput, calls=%fused_computation.17 | convolution fusion | flops 1099956224 | bytes 21561344 | tf_op jit(solution)/shard_map/qhd,khd->hqk/dot_general | solution.py:138
  249.7 10.8 %fusion.52 = f32[16,64,1024]{2,1,0:T(8,128)} fusion(bf16[16,512,1024]{2,1,0:T(8,128)(2,1)} %fusion.9, bf16[1024,16,64]{0,2,1:T(8,128)(2,1)S(1)} %copy-done.14), kind=kOutput, calls=%fused_computation.105 | convolution fusion | flops 1073741824 | bytes 22020096 | tf_op jit(solution)/shard_map/hqk,qhm->khm/dot_general | solution.py:152
  260.5 12.9 %convolution_bitcast_fusion.1 = f32[512,16,64]{0,2,1:T(8,128)} fusion(bf16[1024,16,64]{0,2,1:T(8,128)(2,1)} %copy-done.5, bf16[16,512,1024]{2,1,0:T(8,128)(2,1)} %fusion.9), kind=kOutput, calls=%fused_computation.100 | convolution fusion | flops 1073741824 | bytes 20971520 | tf_op jit(solution)/shard_map/hqk,khm->qhm/dot_general | solution.py:150
  273.5 11.3 %fusion.10 = bf16[16,512,1024]{2,1,0:T(8,128)(2,1)} fusion(f32[16,512]{1,0:T(8,128)S(1)} %bitcast_divide_fusion.2, pred[512,1024]{1,0:T(8,128)(4,1)} %get-tuple-element.51, bf16[1024,16,64]{0,2,1:T(8,128)(2,1)} %bitcast.96, f32[512,16,64]{0,2,1:T(8,128)} %bitcast.97, f32[512,16]{0,1:T(8,128)S(1)} %bitcast.102), kind=kOutput, calls=%fused_computation.18 | convolution fusion | flops 1099956224 | bytes 21561344 | tf_op jit(solution)/shard_map/qhd,khd->hqk/dot_general | solution.py:138
  302.5 13.0 %convolution_bitcast_fusion = f32[512,16,64]{0,2,1:T(8,128)} fusion(bf16[1024,16,64]{0,2,1:T(8,128)(2,1)} %copy-done.5, bf16[16,512,1024]{2,1,0:T(8,128)(2,1)} %fusion.10), kind=kOutput, calls=%fused_computation.99 | convolution fusion | flops 1073741824 | bytes 20971520 | tf_op jit(solution)/shard_map/hqk,khm->qhm/dot_general | solution.py:150
  337.2 11.3 %fusion.18 = f32[16,64,1024]{2,1,0:T(8,128)} fusion(bf16[16,512,1024]{2,1,0:T(8,128)(2,1)} %get-tuple-element.61, pred[512,1024]{1,0:T(8,128)(4,1)S(1)} %copy-done.31, f32[512,16,64]{0,2,1:T(8,128)S(1)} %bitcast.100, f32[512,16]{0,1:T(8,128)S(1)} %bitcast.106), kind=kOutput, calls=%fused_computation.41 | convolution fusion | flops 1083179008 | bytes 23625728 | tf_op jit(solution)/shard_map/hqk,qhd->khd/dot_general | solution.py:146
  348.5 12.4 %add_convert_fusion.2 = bf16[16,64,1024]{2,1,0:T(8,128)(2,1)} fusion(f32[16,64,1024]{2,1,0:T(8,128)} %fusion.18, bf16[16,512,1024]{2,1,0:T(8,128)(2,1)} %get-tuple-element.59, pred[512,1024]{1,0:T(8,128)(4,1)S(1)} %copy-done.29, f32[512,16,64]{0,2,1:T(8,128)} %bitcast.98, f32[512,16]{0,1:T(8,128)S(1)} %bitcast.103), kind=kOutput, calls=%fused_computation.71 | convolution fusion | flops 1085276160 | bytes 25722880 | tf_op jit(solution)/shard_map/hqk,qhd->khd/dot_general | solution.py:146
  361.0 14.8 %fusion.172 = f32[1024,3072]{1,0:T(8,128)} fusion(bf16[1024,1024]{0,1:T(8,128)(2,1)} %bitcast.90, bf16[1024,1024]{0,1:T(8,128)(2,1)} %bitcast.82, bf16[1024,1024]{0,1:T(8,128)(2,1)} %bitcast.85, bf16[1024,1024]{1,0:T(8,128)(2,1)S(1)} %copy-done.7, f32[1024]{0:T(1024)S(1)} %copy-done.44, f32[1024]{0:T(1024)S(1)} %copy-done.41, f32[1024]{0:T(1024)S(1)} %copy-done.39, ...), kind=kOutput, calls=%fused_computation.256 | convolution fusion | flops 6467616768 | bytes 20987904 | tf_op jit(solution)/shard_map/dot_general | solution.py:73
  376.5 39.0 %all-gather = bf16[32,1,128]{2,1,0:T(2,128)(2,1)S(1)} all-gather(bf16[1,1,128]{2,1,0:T(2,128)(2,1)S(1)} %bitcast.109), channel_id=1, replica_groups=mesh['dp'=2,'fsdp'=16] {'dp','fsdp'}, dimensions={0}, use_global_device_ids=true | all-gather | bytes 8448 | tf_op jit(solution)/shard_map/all_gather | solution.py:183
  415.5 49.2 %fusion.2 = (bf16[1024,4096]{1,0:T(8,128)(2,1)S(1)}, f32[1024,4096]{1,0:T(8,128)}) fusion(f32[4096]{0:T(1024)S(1)} %bitcast.107, bf16[1024,4096]{1,0:T(8,128)(2,1)} %all-gather.10.cloned.1.call-done, bf16[1024,1024]{1,0:T(8,128)(2,1)S(1)} %copy-done.7, f32[1024]{0:T(1024)S(1)} %copy-done.44, f32[1024]{0:T(1024)S(1)} %copy-done.41, f32[1024]{0:T(1024)S(1)} %copy-done.39, ...), kind=kOutput, calls=%fused_computation.10 | convolution fusion | flops 8873050112 | bytes 35684352 | tf_op jit(solution)/shard_map/dot_general | solution.py:69
  468.0 11.9 %fusion.187 = f32[4096,1024]{1,0:T(8,128)} fusion(bf16[1024,4096]{1,0:T(8,128)(2,1)S(1)} %get-tuple-element.63, bf16[1024,1024]{1,0:T(8,128)(2,1)S(1)} %copy-done.26), kind=kOutput, calls=%fused_computation.267 | convolution fusion | flops 8589934592 | bytes 27262976 | tf_op jit(solution)/shard_map/dot_general | solution.py:73
  480.0 18.5 %convert_reduce_fusion = (f32[4096]{0:T(1024)S(1)}, bf16[1024,4096]{1,0:T(8,128)(2,1)S(1)}) fusion(f32[1024,4096]{1,0:T(8,128)} %get-tuple-element.64, f32[4096]{0:T(1024)S(1)} %bitcast.108, bf16[1024,1024]{1,0:T(8,128)(2,1)} %get-tuple-element.29, bf16[4096,1024]{1,0:T(8,128)(2,1)} %all-gather.12.cloned.1.call-done), kind=kOutput, calls=%fused_computation.19 | convolution fusion | flops 8644456448 | bytes 35684352 | tf_op jit(solution)/shard_map/dot_general | solution.py:79
  502.3 12.2 %fusion.174 = f32[1024,4096]{1,0:T(8,128)} fusion(bf16[1024,4096]{1,0:T(8,128)(2,1)S(1)} %get-tuple-element.69, bf16[1024,1024]{1,0:T(8,128)(2,1)S(1)} %copy-done.7, f32[1024]{0:T(1024)S(1)} %copy-done.44, f32[1024]{0:T(1024)S(1)} %copy-done.41, f32[1024]{0:T(1024)S(1)} %copy-done.39, f32[1024]{0:T(1024)S(1)} %copy-done.37), kind=kOutput, calls=%fused_computation.258 | convolution fusion | flops 8596226048 | bytes 27279360 | tf_op jit(solution)/shard_map/dot_general | solution.py:73
  524.7 9.6 fusion.173
  534.4 16.8 %fusion.34 = (f32[1024]{0:T(1024)S(1)}, f32[1024]{0:T(1024)S(1)}, f32[1024]{0:T(1024)S(1)}, f32[1024]{0:T(1024)S(1)}, f32[1024,1024]{1,0:T(8,128)}) fusion(bf16[1024,1024]{1,0:T(8,128)(2,1)S(1)} %copy-done.7, f32[1024]{0:T(1024)S(1)} %copy-done.39, f32[1024]{0:T(1024)S(1)} %copy-done.37, f32[1024]{0:T(1024)S(1)} %copy-done.41, ...), kind=kOutput, calls=%fused_computation.57 | convolution fusion | flops 8601464832 | bytes 27291648 | tf_op jit(solution)/shard_map/dot_general | solution.py:79
  551.1 39.7 %all-reduce.16 = (f32[1024]{0:T(1024)S(1)}, f32[1024]{0:T(1024)S(1)}, f32[3072]{0:T(1024)S(1)}, f32[1024]{0:T(1024)S(1)}, f32[4096]{0:T(1024)S(1)}) all-reduce(f32[1024]{0:T(1024)S(1)} %get-tuple-element.12, f32[1024]{0:T(1024)S(1)} %get-tuple-element.15, ...), channel_id=2, replica_groups=mesh['dp'=2,'fsdp'=16] {'dp','fsdp'}, use_global_device_ids=true, to_apply=%region_17.18.clone | all-reduce | flops 10240 | bytes 81920
  599.2 15.1 %fusion.36 = f32[1024,1024]{1,0:T(8,128)} fusion(bf16[1024,1024]{1,0:T(8,128)(2,1)S(1)} %copy-done.7, f32[1024,1024]{1,0:T(8,128)S(1)} %copy-done.57, f32[1024]{0:T(1024)S(1)} %convert_element_type.135, f32[1024]{0:T(1024)S(1)} %convert_element_type.132, bf16[1024,4096]{1,0:T(8,128)(2,1)} %copy-done.58, bf16[4096,1024]{1,0:T(8,128)(2,1)} %all-gather.12.cloned.1.call-done), kind=kOutput, calls=%fused_computation.59 | convolution fusion | flops 8595177472 | bytes 27271168 | tf_op jit(solution)/shard_map/dot_general | solution.py:69
  614.3 173.4 %reduce-scatter.11.cloned.1.call-done = f32[128,1024]{1,0:T(8,128)} async-done(((f32[4096,1024]{1,0:T(8,128)}), f32[128,1024]{1,0:T(8,128)}) %reduce-scatter.11.cloned.1.call-update) | async-done | bytes 524304 | tf_op jit(solution)/shard_map/reduce_scatter | solution.py:317
  787.7 187.2 %reduce-scatter.9.cloned.1.call-done = f32[32,4096]{1,0:T(8,128)} async-done(((f32[1024,4096]{1,0:T(8,128)}), f32[32,4096]{1,0:T(8,128)}) %reduce-scatter.9.cloned.1.call-update) | async-done | bytes 524304 | tf_op jit(solution)/shard_map/reduce_scatter | solution.py:315
  (223 shorter events, 157.5 us)
Async XLA Ops:
  7.2 54.0 %copy-start.49 = (s32[64,64]{1,0:T(8,128)S(1)}, s32[64,64]{1,0:T(8,128)}, u32[]{:S(2)}) copy-start(s32[64,64]{1,0:T(8,128)} %param.28) | copy-start | bytes 49156
  7.3 61.4 %all-gather.8.cloned.1.call-start = ((), (), s32[]{:S(2)}) async-start(), calls=%async_computation.5 | async-start | bytes 2162688 | tf_op jit(solution)/shard_map/all_gather | solution.py:180
  8.0 132.4 %all-gather.6.cloned.1.call-start = ((), (), s32[]{:S(2)}) async-start(), calls=%async_computation.4 | async-start | bytes 6488064 | tf_op jit(solution)/shard_map/all_gather | solution.py:178
  8.7 406.8 %all-gather.10.cloned.1.call-start = ((), (), s32[]{:S(2)}) async-start(), calls=%async_computation.6 | async-start | bytes 8650752 | tf_op jit(solution)/shard_map/all_gather | solution.py:182
  9.5 470.6 %all-gather.12.cloned.1.call-start = ((), (), s32[]{:S(2)}) async-start(), calls=%async_computation.7 | async-start | bytes 8650752 | tf_op jit(solution)/shard_map/all_gather | solution.py:184
  10.0 604.3 %reduce-scatter.7.cloned.1.call-start = ((), (), s32[]{:S(2)}) async-start(), calls=%async_computation.9 | async-start | bytes 4325376 | tf_op jit(solution)/shard_map/reduce_scatter | solution.py:313
  16.3 124.0 %copy-start.36 = (f32[1024]{0:T(1024)}, f32[1024]{0:T(1024)S(1)}, u32[]{:S(2)}) copy-start(f32[1024]{0:T(1024)S(1)} %broadcast_multiply_fusion.4) | copy-start | bytes 12292
  17.1 123.3 %copy-start.38 = (f32[1024]{0:T(1024)}, f32[1024]{0:T(1024)S(1)}, u32[]{:S(2)}) copy-start(f32[1024]{0:T(1024)S(1)} %add_rsqrt_fusion) | copy-start | bytes 12292
  61.0 79.4 %copy-start.40 = (f32[1024]{0:T(1024)}, f32[1024]{0:T(1024)S(1)}, u32[]{:S(2)}) copy-start(f32[1024]{0:T(1024)S(1)} %convert_element_type.116) | copy-start | bytes 12292
  61.0 79.4 %copy-start.43 = (f32[1024]{0:T(1024)}, f32[1024]{0:T(1024)S(1)}, u32[]{:S(2)}) copy-start(f32[1024]{0:T(1024)S(1)} %convert_element_type.117) | copy-start | bytes 12292
  61.2 110.3 %copy-start.32 = (f32[1024,8]{0,1:T(8,128)}, f32[1024,8]{0,1:T(8,128)S(1)}, u32[]{:S(2)}) copy-start(f32[1024,8]{0,1:T(8,128)S(1)} %get-tuple-element.48) | copy-start | bytes 98308
  61.2 110.3 %copy-start.34 = (f32[1024,8]{0,1:T(8,128)}, f32[1024,8]{0,1:T(8,128)S(1)}, u32[]{:S(2)}) copy-start(f32[1024,8]{0,1:T(8,128)S(1)} %get-tuple-element.49) | copy-start | bytes 98308
  182.7 15.1 %copy-start.5 = (bf16[1024,16,64]{0,2,1:T(8,128)(2,1)}, bf16[1024,16,64]{0,2,1:T(8,128)(2,1)S(1)}, u32[]{:S(2)}) copy-start(bf16[1024,16,64]{0,2,1:T(8,128)(2,1)S(1)} %get-tuple-element.54) | copy-start | bytes 6291460
  273.5 340.8 %reduce-scatter.5.cloned.1.call-start = ((), (), s32[]{:S(2)}) async-start(), calls=%async_computation.8 | async-start | bytes 12976128 | tf_op jit(solution)/shard_map/reduce_scatter | solution.py:311
  348.5 12.5 %copy-start.7 = (bf16[1024,1024]{1,0:T(8,128)(2,1)S(1)}, bf16[1024,1024]{1,0:T(8,128)(2,1)}, u32[]{:S(2)}) copy-start(bf16[1024,1024]{1,0:T(8,128)(2,1)} %param.15) | copy-start | bytes 6291460
  348.5 12.5 %copy-start.37 = (f32[1024]{0:T(1024)S(1)}, f32[1024]{0:T(1024)}, u32[]{:S(2)}) copy-start(f32[1024]{0:T(1024)} %copy-done.36) | copy-start | bytes 12292
  348.5 12.5 %copy-start.39 = (f32[1024]{0:T(1024)S(1)}, f32[1024]{0:T(1024)}, u32[]{:S(2)}) copy-start(f32[1024]{0:T(1024)} %copy-done.38) | copy-start | bytes 12292
  348.5 12.5 %copy-start.41 = (f32[1024]{0:T(1024)S(1)}, f32[1024]{0:T(1024)}, u32[]{:S(2)}) copy-start(f32[1024]{0:T(1024)} %copy-done.40) | copy-start | bytes 12292
  348.5 12.5 %copy-start.44 = (f32[1024]{0:T(1024)S(1)}, f32[1024]{0:T(1024)}, u32[]{:S(2)}) copy-start(f32[1024]{0:T(1024)} %copy-done.43) | copy-start | bytes 12292
  375.9 411.8 %reduce-scatter.11.cloned.1.call-start = ((), (), s32[]{:S(2)}) async-start(), calls=%async_computation.11 | async-start | bytes 17301504 | tf_op jit(solution)/shard_map/reduce_scatter | solution.py:317
  415.5 52.5 %copy-start.26 = (bf16[1024,1024]{1,0:T(8,128)(2,1)S(1)}, bf16[1024,1024]{1,0:T(8,128)(2,1)}, u32[]{:S(2)}) copy-start(bf16[1024,1024]{1,0:T(8,128)(2,1)} %get-tuple-element.29) | copy-start | bytes 6291460
  480.0 494.9 %reduce-scatter.9.cloned.1.call-start = ((), (), s32[]{:S(2)}) async-start(), calls=%async_computation.10 | async-start | bytes 17301504 | tf_op jit(solution)/shard_map/reduce_scatter | solution.py:315
  534.4 16.8 %copy-start.42 = (f32[1024]{0:T(1024)S(1)}, f32[1024]{0:T(1024)}, u32[]{:S(2)}) copy-start(f32[1024]{0:T(1024)} %get-tuple-element.28) | copy-start | bytes 12292
  591.5 383.4 %copy-start.55 = (f32[32]{0:T(128)}, f32[32]{0:T(128)S(1)}, u32[]{:S(2)}) copy-start(f32[32]{0:T(128)S(1)} %dynamic-slice.3) | copy-start | bytes 388
  (45 other events, 259.4 us)
Sparse Core Ops, SparseCore 0:
  10.9 57.7 all-gather.7
  71.6 68.7 all-gather.5
  143.2 75.9 all-gather.9
  221.9 76.0 all-gather.11
  300.7 138.9 reduce-scatter.6
  446.2 153.8 reduce-scatter.4
  603.0 184.6 reduce-scatter.10
  790.7 184.1 reduce-scatter.8
where the time goes:
time: 986 us; the launch traced here: 982 us
  waiting for transfers between devices  426 us (43%)
  matrix products  332 us (34%)
  blocking collectives  121 us (12%)
  local copies, waits for them, and re-layouts  49.7 us (5%)
  other arithmetic  37.4 us (4%)
  between operations  15.2 us (2%)
    reduce_scatter x1, waiting for transfers between devices, shards(): lax.psum_scatter(g_up_weight, ('dp', 'fsdp'), scatter_dimension=0, tiled=...  187 us
    reduce_scatter x1, waiting for transfers between devices, shards(): lax.psum_scatter(g_down_weight, ('dp', 'fsdp'), scatter_dimension=0, tile...  173 us
    unnamed x2, blocking collectives  82.3 us
    dot_general x4, matrix products, plain_dot(): return jnp.dot(left, right, preferred_element_type=jnp.float32)  77.8 us
    all_gather x1, waiting for transfers between devices, shards(): lax.all_gather(qkv_weight, ('dp', 'fsdp'), axis=0, tiled=True)  62.4 us
    dot_general x4, matrix products, back_proj(): lax.dot_general(left, right, (((1,), (1,)), ((), ())), preferred_element_...  49.5 us
    dot_general x4, matrix products, outer_sum(): lax.dot_general(left, right, (((0,), (0,)), ((), ())), preferred_element_...  43.3 us
    all_gather x1, blocking collectives, shards(): lax.all_gather(fc1_bias, ('dp', 'fsdp'), axis=0, tiled=True)  39 us
  transfers between devices with their start and end apart: 8, of which 4 were waited for; matrix products, arithmetic and copies ran while one was open for 41% of the time, Pallas kernels for 0%

commit v1 on v0

--- a/solution.py
+++ b/solution.py
@@ -13,6 +13,28 @@
 feature_scale = 0.2
 epsilon = 1e-05
 precise = lax.Precision.HIGHEST
+
+
+def in_order(blocks, dim):
+    shape = list(blocks.shape[1:])
+    shape[dim] *= blocks.shape[0]
+    return jnp.moveaxis(blocks, 0, dim).reshape(shape)
+
+
+def collected_by_bits(x, axis):
+    devices = lax.axis_size(axis)
+    pieces = x[None]
+    for level in range(devices.bit_length() - 1):
+        distance = 1 << level
+        received = lax.ppermute(pieces, axis, [(i, i ^ distance) for i in range(devices)])
+        both = jnp.stack([pieces, received])
+        upper = lax.axis_index(axis) >> level & 1
+        pieces = jnp.where(upper == 0, both, both[::-1]).reshape(-1, *x.shape)
+    return pieces
+
+
+def collect(array, axis, dim):
+    return in_order(collected_by_bits(array, axis), dim)
 
 
 def tables(node_seeds, node_weights):
@@ -175,7 +197,7 @@
     whole = (
         lax.all_gather(ln_gain, ("dp", "fsdp"), axis=0, tiled=True),
         lax.all_gather(ln_bias, ("dp", "fsdp"), axis=0, tiled=True),
-        lax.all_gather(qkv_weight, ("dp", "fsdp"), axis=0, tiled=True),
+        collect(qkv_weight, ("dp", "fsdp"), 0),
         lax.all_gather(qkv_bias, ("dp", "fsdp"), axis=0, tiled=True),
         lax.all_gather(out_weight, ("dp", "fsdp"), axis=0, tiled=True),
         lax.all_gather(out_bias, ("dp", "fsdp"), axis=0, tiled=True),

time: 986 us -> 1070 us (1.085)
  blocking collectives: 121 us -> 179 us
  waiting for transfers between devices: 426 us -> 440 us
    ppermute x0 -> x5, waiting for transfers between devices: none -> 107 us  [collected_by_bits(): lax.ppermute(pieces, axis, [(i, i ^ distance) for i in range(devices)])]
    all_gather x1, waiting for transfers between devices: 62.4 us -> 0.01 us  [shards(): lax.all_gather(qkv_weight, ('dp', 'fsdp'), axis=0, tiled=True)]
    unnamed x2, blocking collectives: 82.3 us -> 140 us
    reduce_scatter x1, waiting for transfers between devices: 173 us -> 142 us  [shards(): lax.psum_scatter(g_down_weight, ('dp', 'fsdp'), scatter_dimension=0, tile...]
  transfers between devices with their start and end apart: 8 -> 13, of which waited for: 4 -> 6; matrix products, arithmetic and copies ran while one was open for 41% -> 38% of each run, Pallas kernels for 0% -> 0%
where the time goes in v1:
time: 1070 us; the launch traced here: 1060 us
  waiting for transfers between devices  440 us (41%)
  matrix products  331 us (31%)
  blocking collectives  179 us (17%)
  local copies, waits for them, and re-layouts  47.7 us (4%)
  other arithmetic  44.8 us (4%)
  between operations  15.3 us (1%)
    reduce_scatter x1, waiting for transfers between devices, shards(): lax.psum_scatter(g_up_weight, ('dp', 'fsdp'), scatter_dimension=0, tiled=...  189 us
    reduce_scatter x1, waiting for transfers between devices, shards(): lax.psum_scatter(g_down_weight, ('dp', 'fsdp'), scatter_dimension=0, tile...  142 us
    unnamed x2, blocking collectives  140 us
    ppermute x5, waiting for transfers between devices, collected_by_bits(): lax.ppermute(pieces, axis, [(i, i ^ distance) for i in range(devices)])  107 us
    dot_general x4, matrix products, plain_dot(): return jnp.dot(left, right, preferred_element_type=jnp.float32)  75.8 us
    dot_general x4, matrix products, back_proj(): lax.dot_general(left, right, (((1,), (1,)), ((), ())), preferred_element_...  49.8 us
    dot_general x4, matrix products, outer_sum(): lax.dot_general(left, right, (((0,), (0,)), ((), ())), preferred_element_...  43.3 us
    all_gather x1, blocking collectives, shards(): lax.all_gather(fc1_bias, ('dp', 'fsdp'), axis=0, tiled=True)  39.5 us
  transfers between devices with their start and end apart: 13, of which 6 were waited for; matrix products, arithmetic and copies ran while one was open for 38% of the time, Pallas kernels for 0%

profile of v1, /device:TPU:4, one launch (start us, length us, event | category | flops | bytes accessed | tf_op | source)
XLA Modules:
  0.0 1063.9 jit_solution(2204393974308437081)
XLA Ops:
  25.7 19.9 %collective-permute-done.2 = bf16[4,32,3072]{2,1,0:T(8,128)(2,1)} collective-permute-done((bf16[4,32,3072]{2,1,0:T(8,128)(2,1)S(1)}, bf16[4,32,3072]{2,1,0:T(8,128)(2,1)}, u32[]{:S(2)}, u32[]{:S(2)}) %collective-permute-start.2) | collective-permute-done | bytes 786464 | tf_op jit(solution)/shard_map/ppermute | solution.py:29
  52.9 94.9 %all-reduce.17 = (bf16[3072]{0:T(1024)(128)(2,1)S(1)}, bf16[1024]{0:T(1024)(128)(2,1)S(1)}, bf16[1024]{0:T(1024)(128)(2,1)S(1)}, bf16[1024]{0:T(1024)(128)(2,1)}, bf16[1024]{0:T(1024)(128)(2,1)}) all-reduce(bf16[3072]{0:T(1024)(128)(2,1)S(1)} %dynamic-update-slice.2, ...), channel_id=1, replica_groups=mesh['dp'=2,'fsdp'=16] {'dp','fsdp'}, use_global_device_ids=true, to_apply=%add.8 | all-reduce | flops 7168 | bytes 28672
  167.8 76.1 %collective-permute-done.4 = bf16[16,32,3072]{2,1,0:T(8,128)(2,1)} collective-permute-done((bf16[16,32,3072]{2,1,0:T(8,128)(2,1)}, bf16[16,32,3072]{2,1,0:T(8,128)(2,1)}, u32[]{:S(2)}, u32[]{:S(2)}) %collective-permute-start.4) | collective-permute-done | bytes 3145760 | tf_op jit(solution)/shard_map/ppermute | solution.py:29
  313.2 13.2 %bitcast_divide_fusion.1 = f32[512,16,64]{0,2,1:T(8,128)} fusion(bf16[1024,16,64]{0,2,1:T(8,128)(2,1)} %bitcast.114, bf16[16,512,1024]{2,1,0:T(8,128)(2,1)} %get-tuple-element.63, pred[512,1024]{1,0:T(8,128)(4,1)} %get-tuple-element.52, f32[512,16]{0,1:T(8,128)S(1)} %bitcast.129), kind=kOutput, calls=%fused_computation.92 | convolution fusion | flops 1082654720 | bytes 21528576 | tf_op jit(solution)/shard_map/hqk,khd->qhd/dot_general | solution.py:134
  326.4 11.9 %multiply_reduce_fusion.3 = (f32[512,16]{0,1:T(8,128)S(1)}, f32[512,16]{0,1:T(8,128)S(1)}, bf16[512,16,64]{0,2,1:T(8,128)(2,1)S(1)}, bf16[512,16,64]{0,2,1:T(8,128)(2,1)S(1)}) fusion(f32[1024,1024]{0,1:T(8,128)} %copy-done.20, f32[512,16,64]{0,2,1:T(8,128)} %bitcast_divide_fusion.1, f32[512,16]{0,1:T(8,128)S(1)} %bitcast.126, ...), kind=kOutput, calls=%fused_computation.93 | convolution fusion | flops 1085784064 | bytes 27885568 | tf_op jit(solution)/shard_map/hqk,khd->qhd/dot_general | solution.py:134
  345.0 11.4 %fusion.9 = bf16[16,512,1024]{2,1,0:T(8,128)(2,1)} fusion(f32[16,512]{1,0:T(8,128)S(1)} %bitcast_divide_fusion.3, pred[512,1024]{1,0:T(8,128)(4,1)} %get-tuple-element.52, bf16[1024,16,64]{0,2,1:T(8,128)(2,1)} %bitcast.116, f32[512,16,64]{0,2,1:T(8,128)} %bitcast.120, f32[512,16]{0,1:T(8,128)S(1)} %bitcast.130), kind=kOutput, calls=%fused_computation.17 | convolution fusion | flops 1099956224 | bytes 21561344 | tf_op jit(solution)/shard_map/qhd,khd->hqk/dot_general | solution.py:160
  356.4 10.9 %fusion.52 = f32[16,64,1024]{2,1,0:T(8,128)} fusion(bf16[16,512,1024]{2,1,0:T(8,128)(2,1)} %fusion.9, bf16[1024,16,64]{0,2,1:T(8,128)(2,1)S(1)} %copy-done.15), kind=kOutput, calls=%fused_computation.112 | convolution fusion | flops 1073741824 | bytes 22020096 | tf_op jit(solution)/shard_map/hqk,qhm->khm/dot_general | solution.py:174
  367.3 13.2 %convolution_bitcast_fusion.1 = f32[512,16,64]{0,2,1:T(8,128)} fusion(bf16[1024,16,64]{0,2,1:T(8,128)(2,1)} %copy-done.5, bf16[16,512,1024]{2,1,0:T(8,128)(2,1)} %fusion.9), kind=kOutput, calls=%fused_computation.105 | convolution fusion | flops 1073741824 | bytes 20971520 | tf_op jit(solution)/shard_map/hqk,khm->qhm/dot_general | solution.py:172
  380.6 11.3 %fusion.10 = bf16[16,512,1024]{2,1,0:T(8,128)(2,1)} fusion(f32[16,512]{1,0:T(8,128)S(1)} %bitcast_divide_fusion.2, pred[512,1024]{1,0:T(8,128)(4,1)} %get-tuple-element.53, bf16[1024,16,64]{0,2,1:T(8,128)(2,1)} %bitcast.117, f32[512,16,64]{0,2,1:T(8,128)} %bitcast.118, f32[512,16]{0,1:T(8,128)S(1)} %bitcast.127), kind=kOutput, calls=%fused_computation.18 | convolution fusion | flops 1099956224 | bytes 21561344 | tf_op jit(solution)/shard_map/qhd,khd->hqk/dot_general | solution.py:160
  409.2 13.0 %convolution_bitcast_fusion = f32[512,16,64]{0,2,1:T(8,128)} fusion(bf16[1024,16,64]{0,2,1:T(8,128)(2,1)} %copy-done.5, bf16[16,512,1024]{2,1,0:T(8,128)(2,1)} %fusion.10), kind=kOutput, calls=%fused_computation.104 | convolution fusion | flops 1073741824 | bytes 20971520 | tf_op jit(solution)/shard_map/hqk,khm->qhm/dot_general | solution.py:172
  444.2 11.3 %fusion.18 = f32[16,64,1024]{2,1,0:T(8,128)} fusion(bf16[16,512,1024]{2,1,0:T(8,128)(2,1)} %get-tuple-element.63, pred[512,1024]{1,0:T(8,128)(4,1)S(1)} %copy-done.29, f32[512,16,64]{0,2,1:T(8,128)S(1)} %bitcast.121, f32[512,16]{0,1:T(8,128)S(1)} %bitcast.131), kind=kOutput, calls=%fused_computation.43 | convolution fusion | flops 1083179008 | bytes 23625728 | tf_op jit(solution)/shard_map/hqk,qhd->khd/dot_general | solution.py:168
  455.5 12.4 %add_convert_fusion.2 = bf16[16,64,1024]{2,1,0:T(8,128)(2,1)} fusion(f32[16,64,1024]{2,1,0:T(8,128)} %fusion.18, bf16[16,512,1024]{2,1,0:T(8,128)(2,1)} %get-tuple-element.61, pred[512,1024]{1,0:T(8,128)(4,1)S(1)} %copy-done.27, f32[512,16,64]{0,2,1:T(8,128)} %bitcast.119, f32[512,16]{0,1:T(8,128)S(1)} %bitcast.128), kind=kOutput, calls=%fused_computation.74 | convolution fusion | flops 1085276160 | bytes 25722880 | tf_op jit(solution)/shard_map/hqk,qhd->khd/dot_general | solution.py:168
  467.9 14.8 %fusion.174 = f32[1024,3072]{1,0:T(8,128)} fusion(bf16[1024,1024]{0,1:T(8,128)(2,1)} %bitcast.111, bf16[1024,1024]{0,1:T(8,128)(2,1)} %bitcast.100, bf16[1024,1024]{0,1:T(8,128)(2,1)} %bitcast.103, bf16[1024,1024]{1,0:T(8,128)(2,1)S(1)} %copy-done.7, f32[1024]{0:T(1024)S(1)} %copy-done.42, f32[1024]{0:T(1024)S(1)} %copy-done.37, f32[1024]{0:T(1024)S(1)} %copy-done.39, ...), kind=kOutput, calls=%fused_computation.268 | convolution fusion | flops 6467616768 | bytes 20987904 | tf_op jit(solution)/shard_map/dot_general | solution.py:95
  483.4 39.5 %all-gather = bf16[32,1,128]{2,1,0:T(2,128)(2,1)S(1)} all-gather(bf16[1,1,128]{2,1,0:T(2,128)(2,1)S(1)} %bitcast.134), channel_id=1, replica_groups=mesh['dp'=2,'fsdp'=16] {'dp','fsdp'}, dimensions={0}, use_global_device_ids=true | all-gather | bytes 8448 | tf_op jit(solution)/shard_map/all_gather | solution.py:205
  522.9 49.1 %fusion.2 = (bf16[1024,4096]{1,0:T(8,128)(2,1)S(1)}, f32[1024,4096]{1,0:T(8,128)}) fusion(f32[4096]{0:T(1024)S(1)} %bitcast.132, bf16[1024,4096]{1,0:T(8,128)(2,1)} %all-gather.8.cloned.1.call-done, bf16[1024,1024]{1,0:T(8,128)(2,1)S(1)} %copy-done.7, f32[1024]{0:T(1024)S(1)} %copy-done.42, f32[1024]{0:T(1024)S(1)} %copy-done.37, f32[1024]{0:T(1024)S(1)} %copy-done.39, ...), kind=kOutput, calls=%fused_computation.10 | convolution fusion | flops 8873050112 | bytes 35684352 | tf_op jit(solution)/shard_map/dot_general | solution.py:91
  575.3 11.9 %fusion.189 = f32[4096,1024]{1,0:T(8,128)} fusion(bf16[1024,4096]{1,0:T(8,128)(2,1)S(1)} %get-tuple-element.65, bf16[1024,1024]{1,0:T(8,128)(2,1)S(1)} %copy-done.24), kind=kOutput, calls=%fused_computation.279 | convolution fusion | flops 8589934592 | bytes 27262976 | tf_op jit(solution)/shard_map/dot_general | solution.py:95
  587.3 18.1 %convert_reduce_fusion = (f32[4096]{0:T(1024)S(1)}, bf16[1024,4096]{1,0:T(8,128)(2,1)S(1)}) fusion(f32[1024,4096]{1,0:T(8,128)} %get-tuple-element.66, f32[4096]{0:T(1024)S(1)} %bitcast.133, bf16[1024,1024]{1,0:T(8,128)(2,1)} %get-tuple-element.29, bf16[4096,1024]{1,0:T(8,128)(2,1)} %all-gather.10.cloned.1.call-done), kind=kOutput, calls=%fused_computation.19 | convolution fusion | flops 8644456448 | bytes 35684352 | tf_op jit(solution)/shard_map/dot_general | solution.py:101
  608.7 12.2 %fusion.176 = f32[1024,4096]{1,0:T(8,128)} fusion(bf16[1024,4096]{1,0:T(8,128)(2,1)S(1)} %get-tuple-element.71, bf16[1024,1024]{1,0:T(8,128)(2,1)S(1)} %copy-done.7, f32[1024]{0:T(1024)S(1)} %copy-done.42, f32[1024]{0:T(1024)S(1)} %copy-done.37, f32[1024]{0:T(1024)S(1)} %copy-done.39, f32[1024]{0:T(1024)S(1)} %copy-done.35), kind=kOutput, calls=%fused_computation.270 | convolution fusion | flops 8596226048 | bytes 27279360 | tf_op jit(solution)/shard_map/dot_general | solution.py:95
  630.8 10.7 %fusion.175 = f32[1024,1024]{1,0:T(8,128)S(1)} fusion(bf16[1024,3072]{1,0:T(8,128)(2,1)} %all-gather.12.cloned.1.call-done, bf16[1024,1024]{0,1:T(8,128)(2,1)} %bitcast.113, bf16[1024,1024]{0,1:T(8,128)(2,1)} %bitcast.102, bf16[1024,1024]{0,1:T(8,128)(2,1)} %bitcast.105), kind=kOutput, calls=%fused_computation.269 | convolution fusion | flops 6461325312 | bytes 16777216 | tf_op jit(solution)/shard_map/dot_general | solution.py:101
  641.5 16.4 %fusion.34 = (f32[1024]{0:T(1024)S(1)}, f32[1024]{0:T(1024)S(1)}, f32[1024]{0:T(1024)S(1)}, f32[1024]{0:T(1024)S(1)}, f32[1024,1024]{1,0:T(8,128)}) fusion(bf16[1024,1024]{1,0:T(8,128)(2,1)S(1)} %copy-done.7, f32[1024]{0:T(1024)S(1)} %copy-done.39, f32[1024]{0:T(1024)S(1)} %copy-done.35, f32[1024]{0:T(1024)S(1)} %copy-done.37, ...), kind=kOutput, calls=%fused_computation.60 | convolution fusion | flops 8601464832 | bytes 27291648 | tf_op jit(solution)/shard_map/dot_general | solution.py:101
  657.9 44.7 %all-reduce.16 = (f32[1024]{0:T(1024)S(1)}, f32[1024]{0:T(1024)S(1)}, f32[3072]{0:T(1024)S(1)}, f32[1024]{0:T(1024)S(1)}, f32[4096]{0:T(1024)S(1)}) all-reduce(f32[1024]{0:T(1024)S(1)} %get-tuple-element.12, f32[1024]{0:T(1024)S(1)} %get-tuple-element.15, ...), channel_id=2, replica_groups=mesh['dp'=2,'fsdp'=16] {'dp','fsdp'}, use_global_device_ids=true, to_apply=%region_17.18.clone | all-reduce | flops 10240 | bytes 81920
  711.0 15.3 %fusion.36 = f32[1024,1024]{1,0:T(8,128)} fusion(bf16[1024,1024]{1,0:T(8,128)(2,1)S(1)} %copy-done.7, f32[1024,1024]{1,0:T(8,128)S(1)} %copy-done.57, f32[1024]{0:T(1024)S(1)} %convert_element_type.135, f32[1024]{0:T(1024)S(1)} %convert_element_type.132, bf16[1024,4096]{1,0:T(8,128)(2,1)} %copy-done.58, bf16[4096,1024]{1,0:T(8,128)(2,1)} %all-gather.10.cloned.1.call-done), kind=kOutput, calls=%fused_computation.62 | convolution fusion | flops 8595177472 | bytes 27271168 | tf_op jit(solution)/shard_map/dot_general | solution.py:91
  726.3 141.6 %reduce-scatter.11.cloned.1.call-done = f32[128,1024]{1,0:T(8,128)} async-done(((f32[4096,1024]{1,0:T(8,128)}), f32[128,1024]{1,0:T(8,128)}) %reduce-scatter.11.cloned.1.call-update) | async-done | bytes 524304 | tf_op jit(solution)/shard_map/reduce_scatter | solution.py:339
  867.9 188.5 %reduce-scatter.9.cloned.1.call-done = f32[32,4096]{1,0:T(8,128)} async-done(((f32[1024,4096]{1,0:T(8,128)}), f32[32,4096]{1,0:T(8,128)}) %reduce-scatter.9.cloned.1.call-update) | async-done | bytes 524304 | tf_op jit(solution)/shard_map/reduce_scatter | solution.py:337
  (243 shorter events, 186.4 us)
Async XLA Ops:
  7.2 153.0 %all-gather.6.cloned.1.call-start = ((), (), s32[]{:S(2)}) async-start(), calls=%async_computation.4 | async-start | bytes 2162688 | tf_op jit(solution)/shard_map/all_gather | solution.py:202
  7.9 515.0 %all-gather.8.cloned.1.call-start = ((), (), s32[]{:S(2)}) async-start(), calls=%async_computation.5 | async-start | bytes 8650752 | tf_op jit(solution)/shard_map/all_gather | solution.py:204
  8.7 578.6 %all-gather.10.cloned.1.call-start = ((), (), s32[]{:S(2)}) async-start(), calls=%async_computation.6 | async-start | bytes 8650752 | tf_op jit(solution)/shard_map/all_gather | solution.py:206
  9.4 621.4 %all-gather.12.cloned.1.call-start = ((), (), s32[]{:S(2)}) async-start(), calls=%async_computation.7 | async-start | bytes 6488064 | tf_op jit(solution)/shard_map/all_gather | solution.py:262
  9.4 1.7 collective-permute-start
  12.2 11.3 %collective-permute-start.1 = (bf16[2,32,3072]{2,1,0:T(8,128)(2,1)S(1)}, bf16[2,32,3072]{2,1,0:T(8,128)(2,1)S(1)}, u32[]{:S(2)}, u32[]{:S(2)}) collective-permute-start(bf16[2,32,3072]{2,1,0:T(8,128)(2,1)S(1)} %get-tuple-element.45), channel_id=1, source_target_pairs={{0,2},{1,3},{2,0},{3,1},{4,6},{5,7},{6,4},{7,5},{8,10},{9,11},{10,... | collective-permute-start | bytes 1179656 | tf_op jit(solution)/shard_map/ppermute | solution.py:29
  23.7 124.1 %copy-start.54 = (s32[64]{0:T(128)S(1)}, s32[64]{0:T(128)}, u32[]{:S(2)}) copy-start(s32[64]{0:T(128)} %param.29) | copy-start | bytes 772
  23.7 124.9 %copy-start.47 = (s32[64,64]{1,0:T(8,128)S(1)}, s32[64,64]{1,0:T(8,128)}, u32[]{:S(2)}) copy-start(s32[64,64]{1,0:T(8,128)} %param.28) | copy-start | bytes 49156
  23.8 125.3 %copy-start.6 = (bf16[1024,1024]{1,0:T(8,128)(2,1)S(1)}, bf16[1024,1024]{1,0:T(8,128)(2,1)}, u32[]{:S(2)}) copy-start(bf16[1024,1024]{1,0:T(8,128)(2,1)} %param.15) | copy-start | bytes 6291460
  23.9 21.6 %collective-permute-start.2 = (bf16[4,32,3072]{2,1,0:T(8,128)(2,1)S(1)}, bf16[4,32,3072]{2,1,0:T(8,128)(2,1)}, u32[]{:S(2)}, u32[]{:S(2)}) collective-permute-start(bf16[4,32,3072]{2,1,0:T(8,128)(2,1)S(1)} %bitcast.107), channel_id=1, source_target_pairs={{0,4},{1,5},{2,6},{3,7},{4,0},{5,1},{6,2},{7,3},{8,12},{9,13},{10,... | collective-permute-start | bytes 2359304 | tf_op jit(solution)/shard_map/ppermute | solution.py:29
  48.3 101.8 %collective-permute-start.3 = (bf16[8,32,3072]{2,1,0:T(8,128)(2,1)}, bf16[8,32,3072]{2,1,0:T(8,128)(2,1)}, u32[]{:S(2)}, u32[]{:S(2)}) collective-permute-start(bf16[8,32,3072]{2,1,0:T(8,128)(2,1)} %bitcast.10), channel_id=1, source_target_pairs={{0,8},{1,9},{2,10},{3,11},{4,12},{5,13},{6,14},{7,15},{8,0},{9,1},... | collective-permute-start | bytes 4718600 | tf_op jit(solution)/shard_map/ppermute | solution.py:29
  51.4 674.9 %reduce-scatter.7.cloned.1.call-start = ((), (), s32[]{:S(2)}) async-start(), calls=%async_computation.9 | async-start | bytes 4325376 | tf_op jit(solution)/shard_map/reduce_scatter | solution.py:335
  147.8 101.4 %copy-start.36 = (f32[1024]{0:T(1024)}, f32[1024]{0:T(1024)S(1)}, u32[]{:S(2)}) copy-start(f32[1024]{0:T(1024)S(1)} %convert_element_type.116) | copy-start | bytes 12292
  147.8 101.4 %copy-start.41 = (f32[1024]{0:T(1024)}, f32[1024]{0:T(1024)S(1)}, u32[]{:S(2)}) copy-start(f32[1024]{0:T(1024)S(1)} %convert_element_type.117) | copy-start | bytes 12292
  154.7 89.2 %collective-permute-start.4 = (bf16[16,32,3072]{2,1,0:T(8,128)(2,1)}, bf16[16,32,3072]{2,1,0:T(8,128)(2,1)}, u32[]{:S(2)}, u32[]{:S(2)}) collective-permute-start(bf16[16,32,3072]{2,1,0:T(8,128)(2,1)} %bitcast.13), channel_id=1, source_target_pairs={{0,16},{1,17},{2,18},{3,19},{4,20},{5,21},{6,22},{7,23},{8,24},{9,... | collective-permute-start | bytes 9437192 | tf_op jit(solution)/shard_map/ppermute | solution.py:29
  154.7 94.5 %copy-start.34 = (f32[1024]{0:T(1024)}, f32[1024]{0:T(1024)S(1)}, u32[]{:S(2)}) copy-start(f32[1024]{0:T(1024)S(1)} %broadcast_multiply_fusion.4) | copy-start | bytes 12292
  155.4 93.8 %copy-start.38 = (f32[1024]{0:T(1024)}, f32[1024]{0:T(1024)S(1)}, u32[]{:S(2)}) copy-start(f32[1024]{0:T(1024)S(1)} %add_rsqrt_fusion) | copy-start | bytes 12292
  155.6 122.7 %copy-start.30 = (f32[1024,8]{0,1:T(8,128)}, f32[1024,8]{0,1:T(8,128)S(1)}, u32[]{:S(2)}) copy-start(f32[1024,8]{0,1:T(8,128)S(1)} %get-tuple-element.50) | copy-start | bytes 98308
  155.7 122.7 %copy-start.32 = (f32[1024,8]{0,1:T(8,128)}, f32[1024,8]{0,1:T(8,128)S(1)}, u32[]{:S(2)}) copy-start(f32[1024,8]{0,1:T(8,128)S(1)} %get-tuple-element.51) | copy-start | bytes 98308
  164.8 79.1 %copy-start.20 = (f32[1024,1024]{0,1:T(8,128)}, f32[1024,1024]{0,1:T(8,128)S(1)}, u32[]{:S(2)}) copy-start(f32[1024,1024]{0,1:T(8,128)S(1)} %fusion.187) | copy-start | bytes 12582916
  380.5 345.8 %reduce-scatter.5.cloned.1.call-start = ((), (), s32[]{:S(2)}) async-start(), calls=%async_computation.8 | async-start | bytes 12976128 | tf_op jit(solution)/shard_map/reduce_scatter | solution.py:333
  482.8 385.1 %reduce-scatter.11.cloned.1.call-start = ((), (), s32[]{:S(2)}) async-start(), calls=%async_computation.11 | async-start | bytes 17301504 | tf_op jit(solution)/shard_map/reduce_scatter | solution.py:339
  587.2 469.2 %reduce-scatter.9.cloned.1.call-start = ((), (), s32[]{:S(2)}) async-start(), calls=%async_computation.10 | async-start | bytes 17301504 | tf_op jit(solution)/shard_map/reduce_scatter | solution.py:337
  703.3 353.1 %copy-start.55 = (f32[32]{0:T(128)}, f32[32]{0:T(128)S(1)}, u32[]{:S(2)}) copy-start(f32[32]{0:T(128)S(1)} %dynamic-slice.3) | copy-start | bytes 388
  (50 other events, 503.0 us)
Sparse Core Ops, SparseCore 0:
  10.8 115.0 all-gather.5
  128.8 95.0 all-gather.7
  226.7 77.9 all-gather.9
  307.5 68.0 all-gather.11
  380.6 140.6 reduce-scatter.6
  527.8 153.0 reduce-scatter.4
  683.8 184.0 reduce-scatter.10
  870.9 185.5 reduce-scatter.8
